TPU v7x, 32 devices: a whole 2x2x4 slice. The times are simulated.
32 devices in a mesh: depth: 2 (over y), vx: 4 (over x, core), vy: 4 (over z).
Axes of the slice: x: 2, y: 2, z: 4, core: 2. Of those that a mesh axis runs over, the one named last changes fastest.
Arguments:
- token_ids: int32 [130], replicated, may hold values from 0 to 8191
- hidden: bfloat16 [2, 128, 7168], P('depth', ('vx', 'vy')), may hold values from -50 to 50
- gain: float32 [2, 7168], P('depth'), may hold values from 0.5 to 1.5
- embedding: bfloat16 [8192, 7168], P('vx', 'vy'), may hold values from -0.6 to 0.6
Outputs:
- row_loss: float32 [128], P(('vx', 'vy'))
All inputs are finite; a program needn't handle non-finite values.
Results may differ from a plain program's by a relative error of at most 0.00044.
Values may be sent and summed in bfloat16 or wider, within the bound.
A program may use at most 128 MiB of HBM per device.

v0:
```python
import jax
import jax.numpy as jnp
from jax import lax
from jax.sharding import PartitionSpec as P

EPS = 1e-06


def combined_all(shard, axis, combine):
    everything = jax.tree.map(lambda part: lax.all_gather(part, axis), shard)
    leading = jax.tree.map(lambda part: part[0], everything)

    def lap(k, so_far):
        return combine(so_far, jax.tree.map(lambda part: part[k], everything))

    return lax.fori_loop(1, lax.axis_size(axis), lap, leading)


def combine(first, second):
    peak = jnp.maximum(first[0], second[0])
    total = first[1] * jnp.exp(first[0] - peak) + second[1] * jnp.exp(second[0] - peak)
    return (peak, total, first[2] + second[2])


def row_stats(logits, wanted, offset):
    peak = jnp.max(logits, axis=1)
    total = jnp.sum(jnp.exp(logits - peak[:, None]), axis=1)
    local = wanted - offset
    columns = lax.broadcasted_iota(jnp.int32, logits.shape, 1)
    picked = jnp.sum(jnp.where(columns == local[:, None], logits, 0.0), axis=1)
    return (peak, total, picked)


def body(token_ids, hidden, gain, embedding):
    head = lax.axis_index("depth")
    rows_dev = hidden.shape[1]
    width = hidden.shape[2]
    groups = lax.axis_size("vx") * lax.axis_size("vy")
    total_rows = rows_dev * groups
    cycle_index = lax.axis_index("vx") * lax.axis_size("vy") + lax.axis_index("vy")
    vocab_local = embedding.shape[0] // lax.axis_size("vy")
    offset = cycle_index * vocab_local
    values = hidden[0].astype(jnp.float32)
    scale = lax.rsqrt(jnp.mean(values * values, axis=1, keepdims=True) + EPS)
    normed = (values * scale * gain[0][None, :]).astype(jnp.bfloat16)
    targets = lax.dynamic_slice_in_dim(token_ids, head + 1, total_rows)
    cols = width // lax.axis_size("vy")
    gathered_all = lax.all_gather(normed, ("vx", "vy"), axis=0, tiled=True)
    gathered = lax.dynamic_slice_in_dim(gathered_all, lax.axis_index("vy") * cols, cols, 1)
    logits_t = lax.psum_scatter(
        lax.dot_general(
            embedding, gathered, (((1,), (1,)), ((), ())), preferred_element_type=jnp.float32
        ),
        "vy",
        scatter_dimension=0,
        tiled=True,
    )
    stats = row_stats(logits_t.T, targets, offset)
    merged = combined_all(stats, ("vx", "vy"), combine)
    peak, total, picked = (
        lax.dynamic_slice_in_dim(item, cycle_index * rows_dev, rows_dev) for item in merged
    )
    loss = peak + jnp.log(total) - picked
    return lax.psum(loss, "depth")


def solution(mesh):
    in_specs = (P(), P("depth", ("vx", "vy"), None), P("depth", None), P("vx", "vy"))
    out_specs = P(("vx", "vy"))
    return jax.shard_map(body, mesh=mesh, in_specs=in_specs, out_specs=out_specs, check_vma=False)
```

profile of v0, /device:TPU:0, one launch (start us, length us, event | category | flops | bytes accessed | tf_op | source)
XLA Modules:
  0.0 189.6 jit_solution(2492664516821674077)
XLA Ops:
  6.5 0.0 copy-start
  6.5 0.0 all-gather.8.cloned.1.call-start
  6.5 1.1 fusion.11
  7.6 1.6 fusion.13
  9.3 0.0 all-gather.8.cloned.1.call-update
  9.3 0.0 reduce-scatter.2.cloned.1.call-start
  9.3 43.6 %all-gather.8.cloned.1.call-done = bf16[128,7168]{1,0:T(8,128)(2,1)} async-done(((bf16[8,7168]{1,0:T(8,128)(2,1)}), bf16[128,7168]{1,0:T(8,128)(2,1)}) %all-gather.8.cloned.1.call-update) | async-done | bytes 1835024 | tf_op jit(solution)/shard_map/all_gather | solution.py:48
  53.0 6.7 %convolution_bitcast_fusion = f32[2048,128]{0,1:T(8,128)} fusion(bf16[2048,1792]{1,0:T(8,128)(2,1)} %param.9, bf16[128,7168]{1,0:T(8,128)(2,1)} %all-gather.8.cloned.1.call-done, s32[]{:T(128)S(6)} %select_n.27), kind=kOutput, calls=%fused_computation.10 | convolution fusion | flops 939524096 | bytes 8847364 | tf_op jit(solution)/shard_map/dot_general | solution.py:51
  59.7 0.0 reduce-scatter.2.cloned.1.call-update
  59.7 0.0 copy-done
  59.7 0.1 dynamic-slice_subtract_fusion.1
  59.8 26.2 %reduce-scatter.2.cloned.1.call-done = f32[512,128]{0,1:T(8,128)} async-done(((f32[2048,128]{0,1:T(8,128)}), f32[512,128]{0,1:T(8,128)}) %reduce-scatter.2.cloned.1.call-update) | async-done | bytes 262160 | tf_op jit(solution)/shard_map/reduce_scatter | solution.py:50
  86.0 1.1 reduce_max.9
  87.1 1.2 fusion.10
  88.3 29.2 %all-gather.5 = f32[16,1,128]{2,1,0:T(1,128)S(1)} all-gather(f32[1,1,128]{2,1,0:T(1,128)S(1)} %bitcast.54), channel_id=4, replica_groups=mesh['depth'=2,'vx'=4,'vy'=4] {'vx','vy'}, dimensions={0}, use_global_device_ids=true | all-gather | bytes 8704 | tf_op jit(solution)/shard_map/all_gather | solution.py:10
  117.4 30.0 %all-gather.4 = f32[16,1,128]{2,1,0:T(1,128)S(1)} all-gather(f32[1,1,128]{2,1,0:T(1,128)S(1)} %bitcast.53), channel_id=3, replica_groups=mesh['depth'=2,'vx'=4,'vy'=4] {'vx','vy'}, dimensions={0}, use_global_device_ids=true | all-gather | bytes 8704 | tf_op jit(solution)/shard_map/all_gather | solution.py:10
  147.4 29.1 %all-gather.3 = f32[16,1,128]{2,1,0:T(1,128)S(1)} all-gather(f32[1,1,128]{2,1,0:T(1,128)S(1)} %bitcast.52), channel_id=2, replica_groups=mesh['depth'=2,'vx'=4,'vy'=4] {'vx','vy'}, dimensions={0}, use_global_device_ids=true | all-gather | bytes 8704 | tf_op jit(solution)/shard_map/all_gather | solution.py:10
  176.6 0.7 while.19
  177.3 0.1 dynamic-slice_subtract_fusion
  177.3 5.4 %psum.7 = f32[8]{0:T(128)} all-reduce(f32[8]{0:T(128)S(1)} %dynamic-slice_subtract_fusion), channel_id=1, replica_groups=mesh['depth'=2,'vx'=4,'vy'=4] {'depth'}, use_global_device_ids=true, to_apply=%region_7.8 | all-reduce | flops 8 | bytes 64 | tf_op jit(solution)/shard_map/psum | solution.py:64
  (19 shorter events, 0.4 us)
Async XLA Ops:
  6.5 53.2 %copy-start = (s32[130]{0:T(256)S(1)}, s32[130]{0:T(256)}, u32[]{:S(2)}) copy-start(s32[130]{0:T(256)} %param.6) | copy-start | bytes 1564
  6.5 46.5 %all-gather.8.cloned.1.call-start = ((), (), s32[]{:S(2)}) async-start(), calls=%async_computation.1 | async-start | bytes 1949696 | tf_op jit(solution)/shard_map/all_gather | solution.py:48
  9.3 76.7 %reduce-scatter.2.cloned.1.call-start = ((), (), s32[]{:S(2)}) async-start(), calls=%async_computation.2 | async-start | bytes 1310720 | tf_op jit(solution)/shard_map/reduce_scatter | solution.py:50
Sparse Core Ops, SparseCore 0:
  9.6 43.3 all-gather.7
  59.8 26.1 reduce-scatter.1
where the time goes:
time: 190 us
  blocking collectives  93.7 us (49%)
  waiting for transfers between devices  69.9 us (37%)
  between operations  13.4 us (7%)
  matrix products  6.69 us (4%)
  other arithmetic  5.53 us (3%)
    all_gather x3, blocking collectives, combined_all(): everything = jax.tree.map(lambda part: lax.all_gather(part, axis), shard)  88.3 us
    all_gather x1, waiting for transfers between devices, body(): gathered_all = lax.all_gather(normed, ('vx', 'vy'), axis=0, tiled=True)  43.6 us
    reduce_scatter x1, waiting for transfers between devices, body(): lax.psum_scatter(lax.dot_general(embedding, gathered, (((1,), (1,)), ((),...  26.2 us
    dot_general x1, matrix products, body(): lax.dot_general(embedding, gathered, (((1,), (1,)), ((), ())), preferred_...  6.69 us
    psum x1, blocking collectives, body(): return lax.psum(loss, 'depth')  5.42 us
  transfers between devices with their start and end apart: 2, of which 2 were waited for; matrix products, arithmetic and copies ran while one was open for 0% of the time, Pallas kernels for 0%

commit v1 on v0

v1 whole, which is shorter than its diff:
```python
import functools

import jax
import jax.numpy as jnp
from jax import lax
from jax.experimental import pallas as pl
from jax.experimental.pallas import tpu as pltpu
from jax.sharding import PartitionSpec as P

EPS = 1e-06
MESH = pl.DeviceIdType.MESH
LANES = 128
TILE = 256
LAG = 2
NT = (((1,), (1,)), ((), ()))


def kernel(
    sizes, tok_ref, hid_ref, gain_ref, emb_hbm, out_ref,
    emb, nx, xg, xall, acc, send_buf, recv_buf, fin, st, rx,
    esem, sa, ra, sb, rb, cs, cr, ss, rs,
):
    heads, nvx, nvy = sizes
    d, i, j = lax.axis_index("depth"), lax.axis_index("vx"), lax.axis_index("vy")
    rows_dev = nx.shape[1]
    cols = nx.shape[2]
    half = emb.shape[0] // 2
    tiles = half // TILE
    pairs = nvx // 2
    pieces = pairs * tiles
    pair_rows = xall.shape[1]

    parts = esem.shape[0]
    block = emb.shape[0] // parts
    loads = [
        pltpu.make_async_copy(
            emb_hbm.at[pl.ds(k * block, block)], emb.at[pl.ds(k * block, block)], esem.at[k]
        )
        for k in range(parts)
    ]
    for load in loads:
        load.start()

    barrier = pltpu.get_barrier_semaphore()
    for k in range(1, nvy):
        pl.semaphore_signal(barrier, inc=1, device_id=(d, i, lax.rem(j + k, nvy)), device_id_type=MESH)
    for k in range(1, nvx):
        pl.semaphore_signal(barrier, inc=1, device_id=(d, lax.rem(i + k, nvx), j), device_id_type=MESH)
    for k in range(1, heads):
        pl.semaphore_signal(barrier, inc=1, device_id=(lax.rem(d + k, heads), i, j), device_id_type=MESH)

    values = hid_ref[0].astype(jnp.float32)
    scale = lax.rsqrt(jnp.mean(values * values, axis=1, keepdims=True) + EPS)
    normed = (values * scale * gain_ref[...]).astype(jnp.bfloat16)
    for k in range(nvy):
        nx[k] = normed[:, k * cols:(k + 1) * cols]
    xg[i, j] = nx[j]
    pl.semaphore_wait(barrier, nvy - 1 + nvx - 1 + heads - 1)

    first = []
    for k in range(1, nvy):
        to = lax.rem(j + k, nvy)
        copy = pltpu.make_async_remote_copy(
            src_ref=nx.at[to], dst_ref=xg.at[i, j], send_sem=sa.at[to], recv_sem=ra.at[j],
            device_id=(d, i, to), device_id_type=MESH,
        )
        copy.start()
        first.append(copy)

    second = []
    for k in range(nvy):
        src = lax.rem(j + k, nvy)
        if k:
            pltpu.make_async_remote_copy(
                src_ref=nx.at[src], dst_ref=xg.at[i, src], send_sem=sa.at[src], recv_sem=ra.at[src],
                device_id=(d, i, src), device_id_type=MESH,
            ).wait_recv()
        for m in range(1, nvx):
            to = lax.rem(i + m, nvx)
            copy = pltpu.make_async_remote_copy(
                src_ref=xg.at[i, src], dst_ref=xg.at[i, src],
                send_sem=sb.at[to, src], recv_sem=rb.at[i, src],
                device_id=(d, to, j), device_id_type=MESH,
            )
            copy.start()
            second.append(copy)

    def ready(p):
        q = lax.rem(i // 2 + p, pairs)

        def arrived(c):
            b = 2 * q + c

            @pl.when(b != i)
            def _():
                for src in range(nvy):
                    pltpu.make_async_remote_copy(
                        src_ref=xg.at[b, src], dst_ref=xg.at[b, src],
                        send_sem=sb.at[b, src], recv_sem=rb.at[b, src],
                        device_id=(d, b, j), device_id_type=MESH,
                    ).wait_recv()

        arrived(0)
        arrived(1)
        both = xg[pl.ds(2 * q, 2)].astype(jnp.float32)
        xall[q] = both.reshape(pair_rows, cols).astype(jnp.bfloat16)

    for load in loads:
        load.wait()

    def hop(way, k, to):
        return pltpu.make_async_remote_copy(
            src_ref=send_buf.at[way, k], dst_ref=recv_buf.at[way, k],
            send_sem=cs.at[way, k], recv_sem=cr.at[way, k],
            device_id=(d, i, to), device_id_type=MESH,
        )

    def advance(way, k, place, to):
        q = lax.rem(i // 2 + k // tiles, pairs)
        t = lax.rem(k, tiles)
        start = pl.multiple_of((1 - way) * half + t * TILE, TILE)
        acc[...] = lax.dot_general(
            xall[q], emb[pl.ds(start, TILE), :], NT, preferred_element_type=jnp.float32
        )

        @pl.when(place > 0)
        def _():
            hop(way, k, to).wait_recv()
            acc[...] += recv_buf[way, k]

        @pl.when(place < nvy - 1)
        def _():
            send_buf[way, k] = acc[...]
            hop(way, k, to).start()

        @pl.when(place == nvy - 1)
        def _():
            fin[q, t] = acc[...]

    up, down = j, nvy - 1 - j
    above, below = jnp.minimum(j + 1, nvy - 1), jnp.maximum(j - 1, 0)
    near = jnp.minimum(up, down)

    def step(s, carry):
        k0 = s - LAG * up
        k1 = s - LAG * down
        p = (s - LAG * near) // tiles

        @pl.when((s >= LAG * near) & (s < LAG * near + pieces) & (lax.rem(s - LAG * near, tiles) == 0))
        def _():
            ready(p)

        @pl.when((k0 >= 0) & (k0 < pieces))
        def _():
            advance(0, k0, up, above)

        @pl.when((k1 >= 0) & (k1 < pieces))
        def _():
            advance(1, k1, down, below)

        return carry

    lax.fori_loop(0, pieces + LAG * (nvy - 1), step, 0)

    at_end = (j == 0) | (j == nvy - 1)
    end = jnp.where(j == 0, 0, 1)
    slot = (d * 2 + end) * nvx + i
    owners = pair_rows // rows_dev

    def stat_copy(head, owner_x, owner_y):
        owner = owner_x * nvy + owner_y
        return pltpu.make_async_remote_copy(
            src_ref=st.at[owner], dst_ref=rx.at[slot],
            send_sem=ss.at[head * nvx * nvy + owner], recv_sem=rs.at[slot],
            device_id=(head, owner_x, owner_y), device_id_type=MESH,
        )

    @pl.when(at_end)
    def _():
        base = (i * 2 + jnp.where(j == 0, 0, 1)) * half
        tok = tok_ref[...].astype(jnp.float32)
        for q in range(pairs):
            logits = fin[q]
            peak = jnp.max(jnp.max(logits, axis=0), axis=1, keepdims=True)
            total = jnp.sum(jnp.sum(jnp.exp(logits - peak[None]), axis=0), axis=1, keepdims=True)
            at = lax.broadcasted_iota(jnp.int32, (pair_rows, tok.shape[1]), 1)
            row = lax.broadcasted_iota(jnp.int32, (pair_rows, tok.shape[1]), 0)
            wanted = jnp.sum(
                jnp.where(at == row + (q * pair_rows + d + 1), tok, 0.0), axis=1, keepdims=True
            )
            column = lax.broadcasted_iota(jnp.int32, (pair_rows, TILE), 1)
            hit = jnp.zeros((pair_rows, TILE), jnp.float32)
            for t in range(tiles):
                here = (column + (base + t * TILE)).astype(jnp.float32)
                hit = hit + jnp.where(here == wanted, logits[t], 0.0)
            picked = jnp.sum(hit, axis=1, keepdims=True)
            lane = lax.broadcasted_iota(jnp.int32, (pair_rows, LANES), 1)
            sub = lax.rem(lax.broadcasted_iota(jnp.int32, (pair_rows, LANES), 0), rows_dev)
            packed = jnp.where(lane == sub, peak, 0.0)
            packed = packed + jnp.where(lane == sub + rows_dev, total, 0.0)
            packed = packed + jnp.where(lane == sub + 2 * rows_dev, picked, 0.0)
            packed = jnp.sum(packed.reshape(owners, rows_dev, LANES), axis=1)
            for o in range(owners):
                st[q * owners + o] = packed[o:o + 1]
        rx[slot] = st[i * nvy + j]
        for head in range(heads):
            for x in range(nvx):
                for y in range(nvy):
                    @pl.when((head != d) | (x != i) | (y != j))
                    def _(head=head, x=x, y=y):
                        stat_copy(head, x, y).start()

    for s in range(heads * 2 * nvx):
        head, rest = divmod(s, 2 * nvx)
        side, x = divmod(rest, nvx)
        y = side * (nvy - 1)

        @pl.when((head != d) | (x != i) | (y != j))
        def _(s=s, head=head, x=x, y=y):
            pltpu.make_async_remote_copy(
                src_ref=st.at[0], dst_ref=rx.at[s], send_sem=ss.at[0], recv_sem=rs.at[s],
                device_id=(head, x, y), device_id_type=MESH,
            ).wait_recv()

    result = jnp.zeros((1, LANES), jnp.float32)
    for head in range(heads):
        block = rx[pl.ds(head * 2 * nvx, 2 * nvx)]
        sums = pltpu.roll(block, LANES - rows_dev, 2)
        picks = pltpu.roll(block, LANES - 2 * rows_dev, 2)
        peak = jnp.max(block, axis=0)
        total = jnp.sum(sums * jnp.exp(block - peak[None]), axis=0)
        result = result + (peak + jnp.log(total) - jnp.sum(picks, axis=0))
    out_ref[...] = result[:, :rows_dev]

    for copy in first + second:
        copy.wait_send()

    def drain(k, carry):
        @pl.when(up < nvy - 1)
        def _():
            hop(0, k, above).wait_send()

        @pl.when(down < nvy - 1)
        def _():
            hop(1, k, below).wait_send()

        return carry

    lax.fori_loop(0, pieces, drain, 0)

    @pl.when(at_end)
    def _():
        for head in range(heads):
            for x in range(nvx):
                for y in range(nvy):
                    @pl.when((head != d) | (x != i) | (y != j))
                    def _(head=head, x=x, y=y):
                        stat_copy(head, x, y).wait_send()


def body(sizes, token_ids, hidden, gain, embedding):
    heads, nvx, nvy = sizes
    rows_dev, width = hidden.shape[1:]
    cols = width // nvy
    pairs = nvx // 2
    pair_rows = 2 * nvy * rows_dev
    tiles = embedding.shape[0] // 2 // TILE
    pieces = pairs * tiles
    dma = pltpu.SemaphoreType.DMA
    vmem = pl.BlockSpec(memory_space=pltpu.VMEM)
    out = pl.pallas_call(
        functools.partial(kernel, sizes),
        out_shape=jax.ShapeDtypeStruct((1, rows_dev), jnp.float32),
        in_specs=[vmem, vmem, vmem, pl.BlockSpec(memory_space=pl.ANY)],
        out_specs=vmem,
        scratch_shapes=[
            pltpu.VMEM(embedding.shape, embedding.dtype),
            pltpu.VMEM((nvy, rows_dev, cols), jnp.bfloat16),
            pltpu.VMEM((nvx, nvy, rows_dev, cols), jnp.bfloat16),
            pltpu.VMEM((pairs, pair_rows, cols), jnp.bfloat16),
            pltpu.VMEM((pair_rows, TILE), jnp.float32),
            pltpu.VMEM((2, pieces, pair_rows, TILE), jnp.float32),
            pltpu.VMEM((2, pieces, pair_rows, TILE), jnp.float32),
            pltpu.VMEM((pairs, tiles, pair_rows, TILE), jnp.float32),
            pltpu.VMEM((nvx * nvy, 1, LANES), jnp.float32),
            pltpu.VMEM((heads * 2 * nvx, 1, LANES), jnp.float32),
            dma((4,)),
            dma((nvy,)),
            dma((nvy,)),
            dma((nvx, nvy)),
            dma((nvx, nvy)),
            dma((2, pieces)),
            dma((2, pieces)),
            dma((heads * nvx * nvy,)),
            dma((heads * 2 * nvx,)),
        ],
        compiler_params=pltpu.CompilerParams(
            collective_id=0, has_side_effects=True, vmem_limit_bytes=62 * 1024 * 1024
        ),
    )(token_ids.reshape(1, -1), hidden, gain, embedding)
    return out.reshape(rows_dev)


def solution(mesh):
    sizes = (mesh.shape["depth"], mesh.shape["vx"], mesh.shape["vy"])
    in_specs = (P(), P("depth", ("vx", "vy"), None), P("depth", None), P("vx", "vy"))
    out_specs = P(("vx", "vy"))
    return jax.shard_map(
        functools.partial(body, sizes), mesh=mesh, in_specs=in_specs, out_specs=out_specs, check_vma=False
    )
```

time: 190 us -> 41 us (0.22)
  blocking collectives: 93.7 us -> 0 us
  waiting for transfers between devices: 69.9 us -> 0 us
  Pallas kernels: 0 us -> 39.6 us
  between operations: 13.4 us -> 0.01 us
  matrix products: 6.69 us -> 0 us
  other arithmetic: 5.53 us -> 0 us
    all_gather x3 -> x0, blocking collectives: 88.3 us -> none  [combined_all(): everything = jax.tree.map(lambda part: lax.all_gather(part, axis), shard)]
    all_gather x1 -> x0, waiting for transfers between devices: 43.6 us -> none  [body(): gathered_all = lax.all_gather(normed, ('vx', 'vy'), axis=0, tiled=True)]
    pallas_call x0 -> x1, Pallas kernels: none -> 39.6 us  [body(): pl.pallas_call(functools.partial(kernel, sizes), out_shape=jax.ShapeDtype...]
    reduce_scatter x1 -> x0, waiting for transfers between devices: 26.2 us -> none  [body(): lax.psum_scatter(lax.dot_general(embedding, gathered, (((1,), (1,)), ((),...]
    dot_general x1 -> x0, matrix products: 6.69 us -> none  [body(): lax.dot_general(embedding, gathered, (((1,), (1,)), ((), ())), preferred_...]
    psum x1 -> x0, blocking collectives: 5.42 us -> none  [body(): return lax.psum(loss, 'depth')]
    reduce_sum x2 -> x0, other arithmetic: 2.25 us -> none  [the longest x1 1.17 us: row_stats(): picked = jnp.sum(jnp.where(columns == local[:, None], logits, 0.0), axis=1)]
  transfers between devices with their start and end apart: 2 -> 0, of which waited for: 2 -> 0; matrix products, arithmetic and copies ran while one was open for 0% -> 0% of each run, Pallas kernels for 0% -> 0%
where the time goes in v1:
time: 41 us; the launch traced here: 40.8 us
  Pallas kernels  39.6 us (97%)
  local copies, waits for them, and re-layouts  1.19 us (3%)
    pallas_call x1, Pallas kernels, body(): pl.pallas_call(functools.partial(kernel, sizes), out_shape=jax.ShapeDtype...  39.6 us
    unnamed x1, local copies, waits for them, and re-layouts  1.19 us

profile of v1, /device:TPU:0, one launch (start us, length us, event | category | flops | bytes accessed | tf_op | source)
XLA Modules:
  0.0 40.8 jit_solution(13450051351947248773)
XLA Ops:
  0.0 39.6 %shard_map.46 = f32[1,8]{1,0:T(1,128)} custom-call(s32[1,130]{1,0:T(1,128)} %bitcast.2, bf16[1,8,7168]{2,1,0:T(8,128)(2,1)} %hid_ref.1, f32[1,7168]{1,0:T(1,128)} %gain_ref.1, bf16[2048,1792]{1,0:T(8,128)(2,1)} %emb_hbm.1), custom_call_target="tpu_custom_call" | custom-call | tf_op jit(solution)/shard_map/pallas_call | solution.py:271
  39.6 1.2 %copy.6 = f32[8]{0:T(128)} copy(f32[8]{0:T(128)} %bitcast.3) | data formatting | bytes 64

commit v2 on v1

--- a/solution.py
+++ b/solution.py
@@ -10,15 +10,17 @@
 EPS = 1e-06
 MESH = pl.DeviceIdType.MESH
 LANES = 128
-TILE = 256
+TILE = 512
 LAG = 2
+TOP = 32767.0
+TINY = 1e-30
 NT = (((1,), (1,)), ((), ()))
 
 
 def kernel(
     sizes, tok_ref, hid_ref, gain_ref, emb_hbm, out_ref,
     emb, nx, xg, xall, acc, send_buf, recv_buf, fin, st, rx,
-    esem, sa, ra, sb, rb, cs, cr, ss, rs,
+    gauge_out, gauge_in, esem, sa, ra, sb, rb, cs, cr, gs, gr, ss, rs,
 ):
     heads, nvx, nvy = sizes
     d, i, j = lax.axis_index("depth"), lax.axis_index("vx"), lax.axis_index("vy")
@@ -115,6 +117,13 @@
             device_id=(d, i, to), device_id_type=MESH,
         )
 
+    def gauge(way, k, to):
+        return pltpu.make_async_remote_copy(
+            src_ref=gauge_out.at[way, k], dst_ref=gauge_in.at[way, k],
+            send_sem=gs.at[way, k], recv_sem=gr.at[way, k],
+            device_id=(d, i, to), device_id_type=MESH,
+        )
+
     def advance(way, k, place, to):
         q = lax.rem(i // 2 + k // tiles, pairs)
         t = lax.rem(k, tiles)
@@ -125,13 +134,18 @@
 
         @pl.when(place > 0)
         def _():
+            gauge(way, k, to).wait_recv()
             hop(way, k, to).wait_recv()
-            acc[...] += recv_buf[way, k]
+            acc[...] += recv_buf[way, k].astype(jnp.float32) * gauge_in[way, k]
 
         @pl.when(place < nvy - 1)
         def _():
-            send_buf[way, k] = acc[...]
+            partial = acc[...]
+            span = jnp.maximum(jnp.max(jnp.abs(partial), axis=0, keepdims=True), TINY)
+            gauge_out[way, k] = span * (1.0 / TOP)
+            send_buf[way, k] = jnp.round(partial * (TOP / span)).astype(jnp.int32).astype(jnp.int16)
             hop(way, k, to).start()
+            gauge(way, k, to).start()
 
         @pl.when(place == nvy - 1)
         def _():
@@ -239,10 +253,12 @@
         @pl.when(up < nvy - 1)
         def _():
             hop(0, k, above).wait_send()
+            gauge(0, k, above).wait_send()
 
         @pl.when(down < nvy - 1)
         def _():
             hop(1, k, below).wait_send()
+            gauge(1, k, below).wait_send()
 
         return carry
 
@@ -279,16 +295,20 @@
             pltpu.VMEM((nvx, nvy, rows_dev, cols), jnp.bfloat16),
             pltpu.VMEM((pairs, pair_rows, cols), jnp.bfloat16),
             pltpu.VMEM((pair_rows, TILE), jnp.float32),
-            pltpu.VMEM((2, pieces, pair_rows, TILE), jnp.float32),
-            pltpu.VMEM((2, pieces, pair_rows, TILE), jnp.float32),
+            pltpu.VMEM((2, pieces, pair_rows, TILE), jnp.int16),
+            pltpu.VMEM((2, pieces, pair_rows, TILE), jnp.int16),
             pltpu.VMEM((pairs, tiles, pair_rows, TILE), jnp.float32),
             pltpu.VMEM((nvx * nvy, 1, LANES), jnp.float32),
             pltpu.VMEM((heads * 2 * nvx, 1, LANES), jnp.float32),
+            pltpu.VMEM((2, pieces, 1, TILE), jnp.float32),
+            pltpu.VMEM((2, pieces, 1, TILE), jnp.float32),
             dma((4,)),
             dma((nvy,)),
             dma((nvy,)),
             dma((nvx, nvy)),
             dma((nvx, nvy)),
+            dma((2, pieces)),
+            dma((2, pieces)),
             dma((2, pieces)),
             dma((2, pieces)),
             dma((heads * nvx * nvy,)),

time: 41 us -> 34.9 us (0.85)
  Pallas kernels: 39.6 us -> 33.6 us
    pallas_call x1, Pallas kernels: 39.6 us -> 33.6 us  [body(): pl.pallas_call(functools.partial(kernel, sizes), out_shape=jax.ShapeDtype...]
where the time goes in v2:
time: 34.9 us; the launch traced here: 34.8 us
  Pallas kernels  33.6 us (96%)
  local copies, waits for them, and re-layouts  1.19 us (3%)
    pallas_call x1, Pallas kernels, body(): pl.pallas_call(functools.partial(kernel, sizes), out_shape=jax.ShapeDtype...  33.6 us
    unnamed x1, local copies, waits for them, and re-layouts  1.19 us

profile of v2, /device:TPU:0, one launch (start us, length us, event | category | flops | bytes accessed | tf_op | source)
XLA Modules:
  0.0 34.8 jit_solution(18165092769189811718)
XLA Ops:
  0.0 33.6 %shard_map.46 = f32[1,8]{1,0:T(1,128)} custom-call(s32[1,130]{1,0:T(1,128)} %bitcast.2, bf16[1,8,7168]{2,1,0:T(8,128)(2,1)} %hid_ref.1, f32[1,7168]{1,0:T(1,128)} %gain_ref.1, bf16[2048,1792]{1,0:T(8,128)(2,1)} %emb_hbm.1), custom_call_target="tpu_custom_call" | custom-call | tf_op jit(solution)/shard_map/pallas_call | solution.py:287
  33.6 1.2 %copy.6 = f32[8]{0:T(128)} copy(f32[8]{0:T(128)} %bitcast.3) | data formatting | bytes 64

commit v3 on v2

--- a/solution.py
+++ b/solution.py
@@ -59,51 +59,61 @@
     xg[i, j] = nx[j]
     pl.semaphore_wait(barrier, nvy - 1 + nvx - 1 + heads - 1)
 
-    first = []
-    for k in range(1, nvy):
-        to = lax.rem(j + k, nvy)
-        copy = pltpu.make_async_remote_copy(
-            src_ref=nx.at[to], dst_ref=xg.at[i, j], send_sem=sa.at[to], recv_sem=ra.at[j],
+    def column_copy(to, src):
+        return pltpu.make_async_remote_copy(
+            src_ref=nx.at[to], dst_ref=xg.at[i, src], send_sem=sa.at[to], recv_sem=ra.at[src],
             device_id=(d, i, to), device_id_type=MESH,
         )
-        copy.start()
-        first.append(copy)
-
-    second = []
-    for k in range(nvy):
-        src = lax.rem(j + k, nvy)
-        if k:
-            pltpu.make_async_remote_copy(
-                src_ref=nx.at[src], dst_ref=xg.at[i, src], send_sem=sa.at[src], recv_sem=ra.at[src],
-                device_id=(d, i, src), device_id_type=MESH,
-            ).wait_recv()
-        for m in range(1, nvx):
-            to = lax.rem(i + m, nvx)
-            copy = pltpu.make_async_remote_copy(
-                src_ref=xg.at[i, src], dst_ref=xg.at[i, src],
-                send_sem=sb.at[to, src], recv_sem=rb.at[i, src],
-                device_id=(d, to, j), device_id_type=MESH,
-            )
-            copy.start()
-            second.append(copy)
+
+    for far in reversed(range(1, nvy)):
+        @pl.when(j + far < nvy)
+        def _(far=far):
+            column_copy(j + far, j).start()
+
+        @pl.when(j - far >= 0)
+        def _(far=far):
+            column_copy(j - far, j).start()
+
+    sibling = i + 1 - 2 * lax.rem(i, 2)
+
+    def slice_copy(b, src, to, sem):
+        return pltpu.make_async_remote_copy(
+            src_ref=xg.at[b, src], dst_ref=xg.at[b, src],
+            send_sem=sb.at[sem, src], recv_sem=rb.at[b, src],
+            device_id=(d, to, j), device_id_type=MESH,
+        )
+
+    def spread(src):
+        for m in range(1, pairs):
+            to = lax.rem(i + 2 * m, nvx)
+            slice_copy(i, src, to, to).start()
+        slice_copy(i, src, sibling, sibling).start()
+
+    spread(j)
+    for far in range(1, nvy):
+        @pl.when(j + far < nvy)
+        def _(far=far):
+            column_copy(j + far, j + far).wait_recv()
+            spread(j + far)
+
+        @pl.when(j - far >= 0)
+        def _(far=far):
+            column_copy(j - far, j - far).wait_recv()
+            spread(j - far)
 
     def ready(p):
         q = lax.rem(i // 2 + p, pairs)
-
-        def arrived(c):
-            b = 2 * q + c
-
-            @pl.when(b != i)
-            def _():
-                for src in range(nvy):
-                    pltpu.make_async_remote_copy(
-                        src_ref=xg.at[b, src], dst_ref=xg.at[b, src],
-                        send_sem=sb.at[b, src], recv_sem=rb.at[b, src],
-                        device_id=(d, b, j), device_id_type=MESH,
-                    ).wait_recv()
-
-        arrived(0)
-        arrived(1)
+        same = 2 * q + lax.rem(i, 2)
+        other = 2 * q + 1 - lax.rem(i, 2)
+
+        @pl.when(p > 0)
+        def _():
+            for src in range(nvy):
+                slice_copy(same, src, sibling, other).wait_recv()
+                slice_copy(same, src, sibling, other).start()
+
+        for src in range(nvy):
+            slice_copy(other, src, other, other).wait_recv()
         both = xg[pl.ds(2 * q, 2)].astype(jnp.float32)
         xall[q] = both.reshape(pair_rows, cols).astype(jnp.bfloat16)
 
@@ -217,12 +227,13 @@
             for o in range(owners):
                 st[q * owners + o] = packed[o:o + 1]
         rx[slot] = st[i * nvy + j]
-        for head in range(heads):
-            for x in range(nvx):
-                for y in range(nvy):
-                    @pl.when((head != d) | (x != i) | (y != j))
-                    def _(head=head, x=x, y=y):
-                        stat_copy(head, x, y).start()
+        for y in range(nvy):
+            for x in reversed(range(nvx)):
+                for head in reversed(range(heads)):
+                    if head or x or y < nvy - 1:
+                        stat_copy(
+                            lax.rem(d + head, heads), lax.rem(i + x, nvx), jnp.where(j == 0, nvy - 1 - y, y)
+                        ).start()
 
     for s in range(heads * 2 * nvx):
         head, rest = divmod(s, 2 * nvx)
@@ -246,8 +257,12 @@
         result = result + (peak + jnp.log(total) - jnp.sum(picks, axis=0))
     out_ref[...] = result[:, :rows_dev]
 
-    for copy in first + second:
-        copy.wait_send()
+    for k in range(1, nvy):
+        column_copy(lax.rem(j + k, nvy), j).wait_send()
+    for k in range(1, nvx):
+        to = lax.rem(i + k, nvx)
+        for src in range(nvy):
+            slice_copy(i, src, to, to).wait_send()
 
     def drain(k, carry):
         @pl.when(up < nvy - 1)
@@ -266,12 +281,13 @@
 
     @pl.when(at_end)
     def _():
-        for head in range(heads):
+        for y in range(nvy):
             for x in range(nvx):
-                for y in range(nvy):
-                    @pl.when((head != d) | (x != i) | (y != j))
-                    def _(head=head, x=x, y=y):
-                        stat_copy(head, x, y).wait_send()
+                for head in range(heads):
+                    if head or x or y < nvy - 1:
+                        stat_copy(
+                            lax.rem(d + head, heads), lax.rem(i + x, nvx), jnp.where(j == 0, nvy - 1 - y, y)
+                        ).wait_send()
 
 
 def body(sizes, token_ids, hidden, gain, embedding):

time: 34.9 us -> 34.7 us (level)
  no operation moved by 1% of the time
where the time goes in v3:
time: 34.7 us; the launch traced here: 34.6 us
  Pallas kernels  33.4 us (96%)
  local copies, waits for them, and re-layouts  1.19 us (3%)
    pallas_call x1, Pallas kernels, body(): pl.pallas_call(functools.partial(kernel, sizes), out_shape=jax.ShapeDtype...  33.4 us
    unnamed x1, local copies, waits for them, and re-layouts  1.19 us

profile of v3, /device:TPU:0, one launch (start us, length us, event | category | flops | bytes accessed | tf_op | source)
XLA Modules:
  0.0 34.6 jit_solution(14363264406185925169)
XLA Ops:
  0.0 33.4 %shard_map.46 = f32[1,8]{1,0:T(1,128)} custom-call(s32[1,130]{1,0:T(1,128)} %bitcast.2, bf16[1,8,7168]{2,1,0:T(8,128)(2,1)} %hid_ref.1, f32[1,7168]{1,0:T(1,128)} %gain_ref.1, bf16[2048,1792]{1,0:T(8,128)(2,1)} %emb_hbm.1), custom_call_target="tpu_custom_call" | custom-call | tf_op jit(solution)/shard_map/pallas_call | solution.py:303
  33.4 1.2 %copy.6 = f32[8]{0:T(128)} copy(f32[8]{0:T(128)} %bitcast.3) | data formatting | bytes 64
